TPU v7x, 256 devices: a whole 4x4x8 slice. The times are simulated.
256 devices in a mesh: tm: 16 (over x_hi, z), tensor: 16 (over x_lo, y, core).
Axes of the slice: x: 4 (x_hi: 2, x_lo: 2; x = x_hi * 2 + x_lo), y: 4, z: 8, core: 2. Of those that a mesh axis runs over, the one named last changes fastest.
Arguments:
- features: bfloat16 [2, 2048, 1536], P(None, 'tm'), may hold values from -6 to 6
- lengths: int32 [2], replicated, may hold values from 512 to 2048, as said below
- norm_gains: float32 [2, 1536], replicated, may hold values from 0.1 to 1.9
- qkv_weight: bfloat16 [3, 1536, 1536], P(None, 'tensor'), may hold values from -0.21650635 to 0.21650635
- pos_weight: bfloat16 [1536, 1536], P('tensor'), may hold values from -0.15625 to 0.15625
- pos_biases: float32 [2, 1536], P(None, 'tensor'), may hold values from -3 to 3
- out_weight: bfloat16 [1536, 1536], P('tensor'), may hold values from -0.15625 to 0.15625
- conv_in_weight: bfloat16 [2, 1536, 1536], P(None, 'tensor'), may hold values from -0.15625 to 0.15625
- depth_kernel: float32 [31, 1536], P(None, 'tensor'), may hold values from -1 to 1
- conv_scale: float32 [1536], P('tensor'), may hold values from 0.1 to 1.9
- conv_shift: float32 [1536], P('tensor'), may hold values from -3 to 3
- conv_out_weight: bfloat16 [1536, 1536], P('tensor'), may hold values from -0.15625 to 0.15625
Outputs:
- encoded: bfloat16 [2, 2048, 1536], P(None, ('tm', 'tensor'))
Inputs may be any that keep to these rules, and one draw needn't show every extreme that they name: `lengths`: the first window is whole.
All inputs are finite; a program needn't handle non-finite values.
Results may differ from a plain program's by a relative error of at most 0.017.
Values may be sent and summed in bfloat16 or wider, within the bound.
A program may use at most 64 MiB of HBM per device.

v0:
```python
import math
import jax
import jax.numpy as jnp
from jax import lax
from jax.sharding import PartitionSpec as P

HD = 96
epsilon = 1e-05


def padded_2(cells, sides, width):
    for axis, dim in sides:
        count = lax.axis_size(axis)
        ends = count - 1
        head = lax.slice_in_dim(cells, 0, width, axis=dim)
        tail = lax.slice_in_dim(cells, cells.shape[dim] - width, cells.shape[dim], axis=dim)
        cells = jnp.concatenate(
            [
                lax.ppermute(tail, axis, [(i, (i + 1) % count) for i in range(ends)]),
                cells,
                lax.ppermute(head, axis, [((i + 1) % count, i) for i in range(ends)]),
            ],
            axis=dim,
        )
    return cells


def layer_norm(values, gain):
    values = values.astype(jnp.float32)
    row_mean = jnp.mean(values, axis=-1, keepdims=True)
    centred = values - row_mean
    variance = jnp.mean(centred * centred, axis=-1, keepdims=True)
    return centred * lax.rsqrt(variance + epsilon) * gain


def positions(offsets, model_width, pos_weight):
    half_width = model_width // 2
    frequency = jnp.exp(
        jnp.arange(half_width, dtype=jnp.float32) * (-2.0 * math.log(10000.0) / model_width)
    )
    angles = offsets.astype(jnp.float32)[:, None] * frequency[None, :]
    pos_table = jnp.concatenate(
        [jnp.sin(angles).astype(jnp.bfloat16), jnp.cos(angles).astype(jnp.bfloat16)], axis=1
    )
    return jnp.einsum(
        "md,cd->mc", pos_table, pos_weight, preferred_element_type=jnp.float32
    ).astype(jnp.bfloat16)


def diagonal_take(pos_table, row_count, col_count):
    table_width = pos_table.shape[-1]
    leading = pos_table.shape[:-2]
    flattened = pos_table.reshape(leading + (row_count * table_width,))
    flattened = lax.slice_in_dim(
        flattened,
        row_count - 1,
        row_count - 1 + row_count * (table_width - 1),
        axis=flattened.ndim - 1,
    )
    return flattened.reshape(leading + (row_count, table_width - 1))[..., :col_count]


def shards(
    features,
    lengths,
    norm_gains,
    qkv_weight,
    pos_weight,
    pos_biases,
    out_weight,
    conv_in_weight,
    depth_kernel,
    conv_scale,
    conv_shift,
    conv_out_weight,
):
    windows, local_rows, model_width = features.shape
    channels = qkv_weight.shape[1]
    heads_here = channels // HD
    score_scale = 1.0 / math.sqrt(HD)
    first_frame = lax.axis_index("tm") * local_rows
    frame_ids = first_frame + jnp.arange(local_rows, dtype=jnp.int32)
    normed = layer_norm(features, norm_gains[0]).astype(jnp.bfloat16)
    projections = jnp.einsum(
        "btd,gcd->btgc", normed, qkv_weight, preferred_element_type=jnp.float32
    )
    query_all = projections[:, :, 0]
    content_q = (
        (query_all + pos_biases[0])
        .astype(jnp.bfloat16)
        .reshape(windows, local_rows, heads_here, HD)
    )
    position_q = (
        (query_all + pos_biases[1])
        .astype(jnp.bfloat16)
        .reshape(windows, local_rows, heads_here, HD)
    )
    key_rows = projections[:, :, 1].astype(jnp.bfloat16)
    value_rows = projections[:, :, 2].astype(jnp.bfloat16)
    global_frames = local_rows * lax.axis_size("tm")
    table_rows = global_frames + local_rows - 1
    all_offsets = first_frame + local_rows - 1 - jnp.arange(table_rows, dtype=jnp.int32)
    relative_all = positions(all_offsets, model_width, pos_weight).reshape(
        table_rows, heads_here, HD
    )
    running_max = jnp.full((windows, heads_here, local_rows), -1e30, jnp.float32)
    key_piece = lax.all_gather(key_rows, "tm", axis=1, tiled=True)
    value_piece = lax.all_gather(value_rows, "tm", axis=1, tiled=True)
    key_count = key_piece.shape[1]
    key_heads = key_piece.reshape(windows, key_count, heads_here, HD)
    value_heads = value_piece.reshape(windows, key_count, heads_here, HD)
    content_scores = jnp.einsum(
        "bqhe,bkhe->bhqk", content_q, key_heads, preferred_element_type=jnp.float32
    )
    full_pos = jnp.einsum(
        "bqhe,mhe->bhqm", position_q, relative_all, preferred_element_type=jnp.float32
    )
    scores = (content_scores + diagonal_take(full_pos, local_rows, key_count)) * score_scale
    key_ids = jnp.arange(key_count, dtype=jnp.int32)
    key_mask = (key_ids[None, :] < lengths[:, None])[:, None, None, :]
    scores = jnp.where(key_mask, scores, -1e30)
    new_max = jnp.maximum(running_max, jnp.max(scores, axis=-1))
    attention_weights = jnp.where(key_mask, jnp.exp(scores - new_max[..., None]), 0.0)
    running_sum = jnp.sum(attention_weights, axis=-1)
    weighted = jnp.einsum(
        "bhqk,bkhe->bhqe",
        attention_weights.astype(jnp.bfloat16),
        value_heads,
        preferred_element_type=jnp.float32,
    )
    head_outputs = (weighted / running_sum[..., None]).astype(jnp.bfloat16)
    head_outputs = head_outputs.transpose(0, 2, 1, 3).reshape(windows, local_rows, channels)
    attention_term = jnp.einsum(
        "btc,cd->btd", head_outputs, out_weight, preferred_element_type=jnp.float32
    )
    row_count = local_rows // lax.axis_size("tensor")
    row_start = lax.axis_index("tensor") * row_count
    attention_full = lax.psum(attention_term.astype(jnp.bfloat16), "tensor").astype(jnp.float32)
    hidden = (features.astype(jnp.float32) + attention_full).astype(jnp.bfloat16)
    hidden_rows = lax.dynamic_slice_in_dim(hidden, row_start, row_count, 1)
    normed_two = layer_norm(hidden, norm_gains[1]).astype(jnp.bfloat16)
    widened = jnp.einsum(
        "btd,gcd->btgc", normed_two, conv_in_weight, preferred_element_type=jnp.float32
    )
    gated_units = widened[:, :, 0] * jax.nn.sigmoid(widened[:, :, 1])
    frame_valid = frame_ids[None, :] < lengths[:, None]
    gated_units = jnp.where(frame_valid[:, :, None], gated_units, 0.0).astype(jnp.bfloat16)
    rim = depth_kernel.shape[0] // 2
    padded = padded_2(gated_units, (("tm", 1),), rim)
    depth_sum = jnp.zeros(gated_units.shape, jnp.float32)
    for tap_index in range(depth_kernel.shape[0]):
        depth_sum = (
            depth_sum
            + padded[:, tap_index : tap_index + local_rows].astype(jnp.float32)
            * depth_kernel[tap_index]
        )
    affine = depth_sum * conv_scale + conv_shift
    activated = (affine * jax.nn.sigmoid(affine)).astype(jnp.bfloat16)
    conv_term = jnp.einsum(
        "btc,cd->btd", activated, conv_out_weight, preferred_element_type=jnp.float32
    )
    conv_rows = lax.psum_scatter(
        conv_term.astype(jnp.bfloat16), "tensor", scatter_dimension=1, tiled=True
    ).astype(jnp.float32)
    return (hidden_rows.astype(jnp.float32) + conv_rows).astype(jnp.bfloat16)


def solution(mesh):
    return jax.shard_map(
        shards,
        mesh=mesh,
        in_specs=(
            P(None, "tm", None),
            P(),
            P(),
            P(None, "tensor", None),
            P("tensor", None),
            P(None, "tensor"),
            P("tensor", None),
            P(None, "tensor", None),
            P(None, "tensor"),
            P("tensor"),
            P("tensor"),
            P("tensor", None),
        ),
        out_specs=P(None, ("tm", "tensor"), None),
        check_vma=False,
    )
```

profile of v0, /device:TPU:4, one launch (start us, length us, event | category | flops | bytes accessed | tf_op | source)
XLA Modules:
  0.0 364.2 jit_solution(17981048727000011265)
XLA Ops:
  6.5 0.8 slice_reduce_fusion
  7.4 1.3 convert_reduce_fusion
  8.7 1.5 fusion.21
  10.2 0.8 slice_bitcast_fusion.32
  11.0 26.0 %fusion = (bf16[2175,768]{1,0:T(8,128)(2,1)}, bf16[2175,768]{1,0:T(8,128)(2,1)}) fusion(f32[768]{0:T(1024)S(1)} %multiply_exponential_fusion, f32[2175]{0:T(1024)S(1)} %subtract_convert_fusion), kind=kLoop, calls=%fused_computation.2 | loop fusion | flops 5011200 | bytes 6693372 | tf_op jit(solution)/shard_map/convert_element_type | solution.py:43
  37.0 0.5 fusion.171
  37.6 0.7 copy-done.3
  38.3 6.8 %convolution_bitcast_fusion = f32[2,1,128,2175]{2,3,0,1:T(8,128)} fusion(bf16[96,1536]{1,0:T(8,128)(2,1)S(1)} %copy-done.7, bf16[2175,768]{1,0:T(8,128)(2,1)} %get-tuple-element.45, bf16[2175,768]{1,0:T(8,128)(2,1)} %get-tuple-element.44, f32[2,128,3,96]{1,3,2,0:T(8,128)S(1)} %get-tuple-element.49, f32[96]{0:T(128)S(1)} %get-tuple-element.47), kind=kOutput, calls=%fused_computation.8 | convolution fusion | flops 761960320 | bytes 9302528 | tf_op jit(solution)/shard_map/bqhe,mhe->bhqm/dot_general | solution.py:115
  45.1 2.0 copy.14
  47.1 4.4 %reshape.176 = f32[2,1,278400]{2,0,1:T(2,128)} reshape(f32[2,1,128,2175]{3,2,0,1:T(8,128)S(1)} %copy.14) | data formatting | bytes 4454400 | tf_op jit(solution)/shard_map/reshape | solution.py:53
  51.5 3.9 %slice.330 = f32[2,1,278272]{2,0,1:T(2,128)S(1)} slice(f32[2,1,278400]{2,0,1:T(2,128)} %reshape.176), slice={[0:2], [0:1], [127:278399]} | slice | bytes 4452352 | tf_op jit(solution)/shard_map/slice | solution.py:54
  55.5 4.5 %reshape.177 = f32[2,1,128,2174]{3,2,0,1:T(8,128)} reshape(f32[2,1,278272]{2,0,1:T(2,128)S(1)} %slice.330) | data formatting | bytes 4452352 | tf_op jit(solution)/shard_map/reshape | solution.py:60
  59.9 46.0 %all-gather = bf16[2,2048,1,96]{1,3,2,0:T(8,128)(2,1)S(1)} all-gather(bf16[2,128,1,96]{1,3,2,0:T(8,128)(2,1)S(1)} %get-tuple-element.10), channel_id=2, replica_groups=mesh['tm'=16,'tensor'=16] {'tm'}, dimensions={1}, use_global_device_ids=true | all-gather | bytes 835584 | tf_op jit(solution)/shard_map/all_gather | solution.py:107
  106.0 2.4 fusion.172
  108.4 42.4 %all-gather.1 = bf16[2,2048,1,96]{1,3,2,0:T(8,128)(2,1)} all-gather(bf16[2,128,1,96]{1,3,2,0:T(8,128)(2,1)S(1)} %get-tuple-element.9), channel_id=3, replica_groups=mesh['tm'=16,'tensor'=16] {'tm'}, dimensions={1}, use_global_device_ids=true | all-gather | bytes 835584 | tf_op jit(solution)/shard_map/all_gather | solution.py:108
  150.9 0.5 fusion.19
  151.4 2.9 convolution_convert_fusion.1
  154.5 122.0 %all-reduce.2.cloned.1.call-done = bf16[2,128,1536]{2,1,0:T(8,128)(2,1)} async-done(((bf16[2,128,1536]{2,1,0:T(8,128)(2,1)}), bf16[2,128,1536]{2,1,0:T(8,128)(2,1)}) %all-reduce.2.cloned.1.call-update) | async-done | bytes 786448 | tf_op jit(solution)/shard_map/psum | solution.py:138
  276.4 1.7 convert_reduce_fusion.1
  278.2 0.3 fusion.24
  278.5 0.5 fusion.49
  279.1 0.1 fusion.170
  279.2 3.5 collective-permute-start
  282.7 6.0 %collective-permute-start.1 = (bf16[2,15,96]{1,2,0:T(8,128)(2,1)S(1)}, bf16[2,15,96]{1,2,0:T(8,128)(2,1)S(1)}, u32[]{:S(2)}, u32[]{:S(2)}) collective-permute-start(bf16[2,15,96]{1,2,0:T(8,128)(2,1)S(1)} %get-tuple-element.12), channel_id=1, source_target_pairs={{16,0},{32,16},{48,32},{64,48},{80,64},{96,80},{112,96},{128,112},... | collective-permute-start | bytes 17288 | tf_op jit(solution)/shard_map/ppermute | solution.py:21
  288.7 0.1 collective-permute-done
  288.8 1.6 collective-permute-done.1
  290.4 1.7 convolution_convert_fusion
  292.1 0.8 copy.17
  292.9 1.0 copy.19
  293.9 62.0 %reduce-scatter.4.cloned.1.call-done = bf16[8,3072]{1,0:T(8,128)(2,1)} async-done(((bf16[128,3072]{1,0:T(8,128)(2,1)}), bf16[8,3072]{1,0:T(8,128)(2,1)}) %reduce-scatter.4.cloned.1.call-update) | async-done | bytes 49168
  355.9 0.8 reshape.190
  356.7 0.6 add_convert_fusion
  (39 shorter events, 0.4 us)
Async XLA Ops:
  6.5 30.5 %copy-start = (bf16[3,96,1536]{2,1,0:T(8,128)(2,1)S(1)}, bf16[3,96,1536]{2,1,0:T(8,128)(2,1)}, u32[]{:S(2)}) copy-start(bf16[3,96,1536]{2,1,0:T(8,128)(2,1)} %param.15) | copy-start | bytes 2654212
  6.5 269.9 %all-reduce.2.cloned.1.call-start = ((), (), s32[]{:S(2)}) async-start(), calls=%async_computation.1 | async-start | bytes 1572864 | tf_op jit(solution)/shard_map/psum | solution.py:138
  11.0 26.0 %copy-start.1 = (bf16[2,128,1536]{2,1,0:T(8,128)(2,1)S(1)}, bf16[2,128,1536]{2,1,0:T(8,128)(2,1)}, u32[]{:S(2)}) copy-start(bf16[2,128,1536]{2,1,0:T(8,128)(2,1)} %param.12) | copy-start | bytes 2359300
  37.0 1.3 copy-start.7
  37.6 0.7 copy-start.3
  55.4 50.5 %copy-start.5 = (s32[2]{0:T(128)S(1)}, s32[2]{0:T(128)}, u32[]{:S(2)}) copy-start(s32[2]{0:T(128)} %param.13) | copy-start | bytes 28
  108.4 43.0 %copy-start.2 = (bf16[96,1536]{1,0:T(8,128)(2,1)S(1)}, bf16[96,1536]{1,0:T(8,128)(2,1)}, u32[]{:S(2)}) copy-start(bf16[96,1536]{1,0:T(8,128)(2,1)} %param.18) | copy-start | bytes 884740
  151.4 3.1 copy-start.4
  154.3 124.2 %copy-start.6 = (bf16[2,96,1536]{2,1,0:T(8,128)(2,1)S(1)}, bf16[2,96,1536]{2,1,0:T(8,128)(2,1)}, u32[]{:S(2)}) copy-start(bf16[2,96,1536]{2,1,0:T(8,128)(2,1)} %param.19) | copy-start | bytes 1769476
  154.3 201.6 %reduce-scatter.4.cloned.1.call-start = ((), (), s32[]{:S(2)}) async-start(), calls=%async_computation.2 | async-start | bytes 835584
  278.1 12.3 %copy-start.8 = (bf16[96,1536]{1,0:T(8,128)(2,1)S(1)}, bf16[96,1536]{1,0:T(8,128)(2,1)}, u32[]{:S(2)}) copy-start(bf16[96,1536]{1,0:T(8,128)(2,1)} %param.23) | copy-start | bytes 884740
  278.1 12.3 %copy-start.9 = (f32[96]{0:T(128)S(1)}, f32[96]{0:T(128)}, u32[]{:S(2)}) copy-start(f32[96]{0:T(128)} %param.22) | copy-start | bytes 1156
  278.1 12.3 %copy-start.10 = (f32[96]{0:T(128)S(1)}, f32[96]{0:T(128)}, u32[]{:S(2)}) copy-start(f32[96]{0:T(128)} %param.21) | copy-start | bytes 1156
  279.2 9.6 %collective-permute-start = (bf16[2,15,96]{1,2,0:T(8,128)(2,1)S(1)}, bf16[2,15,96]{1,2,0:T(8,128)(2,1)S(1)}, u32[]{:S(2)}, u32[]{:S(2)}) collective-permute-start(bf16[2,15,96]{1,2,0:T(8,128)(2,1)S(1)} %get-tuple-element.11), channel_id=1, source_target_pairs={{0,16},{16,32},{32,48},{48,64},{64,80},{80,96},{96,112},{112,128},... | collective-permute-start | bytes 17288 | tf_op jit(solution)/shard_map/ppermute | solution.py:19
  282.7 7.7 %collective-permute-start.1 = (bf16[2,15,96]{1,2,0:T(8,128)(2,1)S(1)}, bf16[2,15,96]{1,2,0:T(8,128)(2,1)S(1)}, u32[]{:S(2)}, u32[]{:S(2)}) collective-permute-start(bf16[2,15,96]{1,2,0:T(8,128)(2,1)S(1)} %get-tuple-element.12), channel_id=1, source_target_pairs={{16,0},{32,16},{48,32},{64,48},{80,64},{96,80},{112,96},{128,112},... | collective-permute-start | bytes 17288 | tf_op jit(solution)/shard_map/ppermute | solution.py:21
Sparse Core Ops, SparseCore 0:
  154.4 121.9 all-reduce.1
  294.0 61.8 reduce-scatter.3
where the time goes:
time: 365 us; the launch traced here: 364 us
  waiting for transfers between devices  186 us (51%)
  blocking collectives  88.5 us (24%)
  other arithmetic  32.2 us (9%)
  local copies, waits for them, and re-layouts  19.9 us (5%)
  matrix products  14.8 us (4%)
  between operations  13.6 us (4%)
  starting transfers between devices  9.5 us (3%)
    psum x1, waiting for transfers between devices, shards(): lax.psum(attention_term.astype(jnp.bfloat16), 'tensor').astype(jnp.float32)  122 us
    unnamed x3, waiting for transfers between devices  62 us
    all_gather x1, blocking collectives, shards(): key_piece = lax.all_gather(key_rows, 'tm', axis=1, tiled=True)  46 us
    all_gather x1, blocking collectives, shards(): value_piece = lax.all_gather(value_rows, 'tm', axis=1, tiled=True)  42.4 us
    convert_element_type x1, other arithmetic, positions(): jnp.sin(angles).astype(jnp.bfloat16)  26 us
  transfers between devices with their start and end apart: 4, of which 4 were waited for; matrix products, arithmetic and copies ran while one was open for 0% of the time, Pallas kernels for 0%

commit v1 on v0

--- a/solution.py
+++ b/solution.py
@@ -6,6 +6,10 @@
 
 HD = 96
 epsilon = 1e-05
+
+
+def divide_column_on(array_in, link_axis="tensor"):
+    return jnp.sum(lax.all_gather(array_in, link_axis), axis=0)
 
 
 def padded_2(cells, sides, width):
@@ -135,7 +139,7 @@
     )
     row_count = local_rows // lax.axis_size("tensor")
     row_start = lax.axis_index("tensor") * row_count
-    attention_full = lax.psum(attention_term.astype(jnp.bfloat16), "tensor").astype(jnp.float32)
+    attention_full = divide_column_on(attention_term.astype(jnp.bfloat16)).astype(jnp.float32)
     hidden = (features.astype(jnp.float32) + attention_full).astype(jnp.bfloat16)
     hidden_rows = lax.dynamic_slice_in_dim(hidden, row_start, row_count, 1)
     normed_two = layer_norm(hidden, norm_gains[1]).astype(jnp.bfloat16)

time: 365 us -> 323 us (0.88)
  waiting for transfers between devices: 186 us -> 138 us
  other arithmetic: 32.2 us -> 37.6 us
    psum x1 -> x0, waiting for transfers between devices: 122 us -> none  [shards(): lax.psum(attention_term.astype(jnp.bfloat16), 'tensor').astype(jnp.float32)]
    all_gather x0 -> x1, waiting for transfers between devices: none -> 73.1 us  [divide_column_on(): return jnp.sum(lax.all_gather(array_in, link_axis), axis=0)]
    reduce_sum x0 -> x1, other arithmetic: none -> 6.66 us  [divide_column_on(): return jnp.sum(lax.all_gather(array_in, link_axis), axis=0)]
where the time goes in v1:
time: 323 us; the launch traced here: 322 us
  waiting for transfers between devices  138 us (43%)
  blocking collectives  88.7 us (27%)
  other arithmetic  37.6 us (12%)
  local copies, waits for them, and re-layouts  20.2 us (6%)
  matrix products  14.8 us (5%)
  between operations  13.7 us (4%)
  starting transfers between devices  9.5 us (3%)
    all_gather x1, waiting for transfers between devices, divide_column_on(): return jnp.sum(lax.all_gather(array_in, link_axis), axis=0)  73.1 us
    unnamed x3, waiting for transfers between devices  63 us
    all_gather x1, blocking collectives, shards(): key_piece = lax.all_gather(key_rows, 'tm', axis=1, tiled=True)  46 us
    all_gather x1, blocking collectives, shards(): value_piece = lax.all_gather(value_rows, 'tm', axis=1, tiled=True)  42.7 us
    convert_element_type x1, other arithmetic, positions(): jnp.sin(angles).astype(jnp.bfloat16)  26 us
    dot_general x1, matrix products, shards(): jnp.einsum('bqhe,mhe->bhqm', position_q, relative_all, preferred_element_...  6.82 us
    reduce_sum x1, other arithmetic, divide_column_on(): return jnp.sum(lax.all_gather(array_in, link_axis), axis=0)  6.66 us
  transfers between devices with their start and end apart: 4, of which 4 were waited for; matrix products, arithmetic and copies ran while one was open for 0% of the time, Pallas kernels for 0%

profile of v1, /device:TPU:4, one launch (start us, length us, event | category | flops | bytes accessed | tf_op | source)
XLA Modules:
  0.0 322.4 jit_solution(2613347406243466659)
XLA Ops:
  6.5 0.8 slice_reduce_fusion
  7.4 1.3 convert_reduce_fusion
  8.7 1.5 fusion.21
  10.2 0.8 slice_bitcast_fusion.32
  11.0 26.0 %fusion = (bf16[2175,768]{1,0:T(8,128)(2,1)}, bf16[2175,768]{1,0:T(8,128)(2,1)}) fusion(f32[768]{0:T(1024)S(1)} %multiply_exponential_fusion, f32[2175]{0:T(1024)S(1)} %subtract_convert_fusion), kind=kLoop, calls=%fused_computation.2 | loop fusion | flops 5011200 | bytes 6693372 | tf_op jit(solution)/shard_map/convert_element_type | solution.py:47
  37.1 0.5 fusion.171
  37.6 0.7 copy-done.4
  38.3 6.8 %convolution_bitcast_fusion = f32[2,1,128,2175]{2,3,0,1:T(8,128)} fusion(bf16[96,1536]{1,0:T(8,128)(2,1)S(1)} %copy-done.8, bf16[2175,768]{1,0:T(8,128)(2,1)} %get-tuple-element.45, bf16[2175,768]{1,0:T(8,128)(2,1)} %get-tuple-element.44, f32[2,128,3,96]{1,3,2,0:T(8,128)S(1)} %get-tuple-element.49, f32[96]{0:T(128)S(1)} %get-tuple-element.47), kind=kOutput, calls=%fused_computation.8 | convolution fusion | flops 761960320 | bytes 9302528 | tf_op jit(solution)/shard_map/bqhe,mhe->bhqm/dot_general | solution.py:119
  45.1 2.0 copy.14
  47.2 4.4 %reshape.176 = f32[2,1,278400]{2,0,1:T(2,128)} reshape(f32[2,1,128,2175]{3,2,0,1:T(8,128)S(1)} %copy.14) | data formatting | bytes 4454400 | tf_op jit(solution)/shard_map/reshape | solution.py:57
  51.5 3.9 %slice.330 = f32[2,1,278272]{2,0,1:T(2,128)S(1)} slice(f32[2,1,278400]{2,0,1:T(2,128)} %reshape.176), slice={[0:2], [0:1], [127:278399]} | slice | bytes 4452352 | tf_op jit(solution)/shard_map/slice | solution.py:58
  55.5 4.5 %reshape.177 = f32[2,1,128,2174]{3,2,0,1:T(8,128)} reshape(f32[2,1,278272]{2,0,1:T(2,128)S(1)} %slice.330) | data formatting | bytes 4452352 | tf_op jit(solution)/shard_map/reshape | solution.py:64
  60.0 46.0 %all-gather = bf16[2,2048,1,96]{1,3,2,0:T(8,128)(2,1)S(1)} all-gather(bf16[2,128,1,96]{1,3,2,0:T(8,128)(2,1)S(1)} %get-tuple-element.10), channel_id=2, replica_groups=mesh['tm'=16,'tensor'=16] {'tm'}, dimensions={1}, use_global_device_ids=true | all-gather | bytes 835584 | tf_op jit(solution)/shard_map/all_gather | solution.py:111
  106.1 2.4 fusion.172
  108.4 42.7 %all-gather.1 = bf16[2,2048,1,96]{1,3,2,0:T(8,128)(2,1)} all-gather(bf16[2,128,1,96]{1,3,2,0:T(8,128)(2,1)S(1)} %get-tuple-element.9), channel_id=3, replica_groups=mesh['tm'=16,'tensor'=16] {'tm'}, dimensions={1}, use_global_device_ids=true | all-gather | bytes 835584 | tf_op jit(solution)/shard_map/all_gather | solution.py:112
  151.1 0.5 fusion.19
  151.7 2.9 convolution_convert_fusion.1
  154.8 73.1 %all-gather.5.cloned.1.call-done = bf16[32,128,1536]{2,1,0:T(8,128)(2,1)} async-done(((bf16[2,128,1536]{2,1,0:T(8,128)(2,1)}), bf16[32,128,1536]{2,1,0:T(8,128)(2,1)}) %all-gather.5.cloned.1.call-update) | async-done | bytes 12582928 | tf_op jit(solution)/shard_map/all_gather | solution.py:12
  227.9 6.7 %reduce_sum.60 = bf16[2,128,1536]{2,1,0:T(8,128)(2,1)S(1)} reduce(bf16[16,2,128,1536]{3,2,1,0:T(8,128)(2,1)} %bitcast.147, bf16[]{:T(256)} %constant.36.clone.1), dimensions={0}, to_apply=%region_4.5 | reduce | flops 5898240 | bytes 13369346 | tf_op jit(solution)/shard_map/reduce_sum | solution.py:12
  234.6 0.3 convert_reduce_fusion.1
  234.9 0.3 fusion.24
  235.3 0.3 copy-done.7
  235.6 0.5 fusion.49
  236.3 3.5 %collective-permute-start = (bf16[2,15,96]{1,2,0:T(8,128)(2,1)S(1)}, bf16[2,15,96]{1,2,0:T(8,128)(2,1)S(1)}, u32[]{:S(2)}, u32[]{:S(2)}) collective-permute-start(bf16[2,15,96]{1,2,0:T(8,128)(2,1)S(1)} %get-tuple-element.11), channel_id=1, source_target_pairs={{0,16},{16,32},{32,48},{48,64},{64,80},{80,96},{96,112},{112,128},... | collective-permute-start | bytes 17288 | tf_op jit(solution)/shard_map/ppermute | solution.py:23
  239.8 6.0 %collective-permute-start.1 = (bf16[2,15,96]{1,2,0:T(8,128)(2,1)S(1)}, bf16[2,15,96]{1,2,0:T(8,128)(2,1)S(1)}, u32[]{:S(2)}, u32[]{:S(2)}) collective-permute-start(bf16[2,15,96]{1,2,0:T(8,128)(2,1)S(1)} %get-tuple-element.12), channel_id=1, source_target_pairs={{16,0},{32,16},{48,32},{64,48},{80,64},{96,80},{112,96},{128,112},... | collective-permute-start | bytes 17288 | tf_op jit(solution)/shard_map/ppermute | solution.py:25
  245.9 1.6 collective-permute-done.1
  247.5 1.7 convolution_convert_fusion
  249.2 0.8 copy.17
  250.0 1.0 copy.19
  251.1 63.0 %reduce-scatter.4.cloned.1.call-done = bf16[8,3072]{1,0:T(8,128)(2,1)} async-done(((bf16[128,3072]{1,0:T(8,128)(2,1)}), bf16[8,3072]{1,0:T(8,128)(2,1)}) %reduce-scatter.4.cloned.1.call-update) | async-done | bytes 49168
  314.0 0.8 reshape.191
  314.9 0.6 add_convert_fusion
  (42 shorter events, 0.6 us)
Async XLA Ops:
  6.5 30.5 %copy-start = (bf16[3,96,1536]{2,1,0:T(8,128)(2,1)S(1)}, bf16[3,96,1536]{2,1,0:T(8,128)(2,1)}, u32[]{:S(2)}) copy-start(bf16[3,96,1536]{2,1,0:T(8,128)(2,1)} %param.15) | copy-start | bytes 2654212
  6.5 221.4 %all-gather.5.cloned.1.call-start = ((), (), s32[]{:S(2)}) async-start(), calls=%async_computation.1 | async-start | bytes 13369344 | tf_op jit(solution)/shard_map/all_gather | solution.py:12
  11.0 26.0 %copy-start.1 = (bf16[2,128,1536]{2,1,0:T(8,128)(2,1)S(1)}, bf16[2,128,1536]{2,1,0:T(8,128)(2,1)}, u32[]{:S(2)}) copy-start(bf16[2,128,1536]{2,1,0:T(8,128)(2,1)} %param.12) | copy-start | bytes 2359300
  37.0 1.3 copy-start.8
  37.6 0.7 copy-start.4
  55.5 50.5 %copy-start.6 = (s32[2]{0:T(128)S(1)}, s32[2]{0:T(128)}, u32[]{:S(2)}) copy-start(s32[2]{0:T(128)} %param.13) | copy-start | bytes 28
  108.4 43.2 %copy-start.3 = (bf16[96,1536]{1,0:T(8,128)(2,1)S(1)}, bf16[96,1536]{1,0:T(8,128)(2,1)}, u32[]{:S(2)}) copy-start(bf16[96,1536]{1,0:T(8,128)(2,1)} %param.18) | copy-start | bytes 884740
  151.7 3.1 copy-start.5
  154.6 159.4 %reduce-scatter.4.cloned.1.call-start = ((), (), s32[]{:S(2)}) async-start(), calls=%async_computation.2 | async-start | bytes 835584
  227.9 6.7 %copy-start.2 = (bf16[2,128,1536]{2,1,0:T(8,128)(2,1)S(1)}, bf16[2,128,1536]{2,1,0:T(8,128)(2,1)}, u32[]{:S(2)}) copy-start(bf16[2,128,1536]{2,1,0:T(8,128)(2,1)} %param.12) | copy-start | bytes 2359300
  234.6 1.1 copy-start.7
  234.9 12.6 %copy-start.9 = (bf16[96,1536]{1,0:T(8,128)(2,1)S(1)}, bf16[96,1536]{1,0:T(8,128)(2,1)}, u32[]{:S(2)}) copy-start(bf16[96,1536]{1,0:T(8,128)(2,1)} %param.23) | copy-start | bytes 884740
  234.9 12.6 %copy-start.10 = (f32[96]{0:T(128)S(1)}, f32[96]{0:T(128)}, u32[]{:S(2)}) copy-start(f32[96]{0:T(128)} %param.22) | copy-start | bytes 1156
  234.9 12.6 %copy-start.11 = (f32[96]{0:T(128)S(1)}, f32[96]{0:T(128)}, u32[]{:S(2)}) copy-start(f32[96]{0:T(128)} %param.21) | copy-start | bytes 1156
  236.3 9.6 %collective-permute-start = (bf16[2,15,96]{1,2,0:T(8,128)(2,1)S(1)}, bf16[2,15,96]{1,2,0:T(8,128)(2,1)S(1)}, u32[]{:S(2)}, u32[]{:S(2)}) collective-permute-start(bf16[2,15,96]{1,2,0:T(8,128)(2,1)S(1)} %get-tuple-element.11), channel_id=1, source_target_pairs={{0,16},{16,32},{32,48},{48,64},{64,80},{80,96},{96,112},{112,128},... | collective-permute-start | bytes 17288 | tf_op jit(solution)/shard_map/ppermute | solution.py:23
  239.8 7.7 %collective-permute-start.1 = (bf16[2,15,96]{1,2,0:T(8,128)(2,1)S(1)}, bf16[2,15,96]{1,2,0:T(8,128)(2,1)S(1)}, u32[]{:S(2)}, u32[]{:S(2)}) collective-permute-start(bf16[2,15,96]{1,2,0:T(8,128)(2,1)S(1)} %get-tuple-element.12), channel_id=1, source_target_pairs={{16,0},{32,16},{48,32},{64,48},{80,64},{96,80},{112,96},{128,112},... | collective-permute-start | bytes 17288 | tf_op jit(solution)/shard_map/ppermute | solution.py:25
Sparse Core Ops, SparseCore 0:
  154.8 73.0 all-gather.4
  251.2 62.8 reduce-scatter.3
